TPU v7x, 256 devices: a whole 4x4x8 slice. The times are simulated.
256 devices in a mesh: depth: 4 (over x), row: 16 (over z, y_hi), col: 4 (over y_lo, core).
Axes of the slice: x: 4, y: 4 (y_hi: 2, y_lo: 2; y = y_hi * 2 + y_lo), z: 8, core: 2. Of those that a mesh axis runs over, the one named last changes fastest.
Arguments:
- tokens: bfloat16 [768, 8192], P(('depth', 'row')), may hold values from -6 to 6
- out_grad: bfloat16 [768, 8192], P(('depth', 'row')), may hold values from -0.59765625 to 0.59765625
- gate_weight: bfloat16 [8192, 16384], P('depth', ('row', 'col')), may hold values from -0.0625 to 0.0625
- up_weight: bfloat16 [8192, 16384], P('depth', ('row', 'col')), may hold values from -0.0625 to 0.0625
- down_weight: bfloat16 [16384, 8192], P(('row', 'col'), 'depth'), may hold values from -0.046875 to 0.046875
Outputs:
- input_grad: bfloat16 [768, 8192], P(('depth', 'row', 'col'))
- gate_grad: bfloat16 [8192, 16384], P('depth', ('row', 'col'))
- up_grad: bfloat16 [8192, 16384], P('depth', ('row', 'col'))
- down_grad: bfloat16 [16384, 8192], P(('row', 'col'), 'depth')
All inputs are finite; a program needn't handle non-finite values.
Results may differ from a plain program's by a relative error of at most 0.024.
Values may be sent and summed in bfloat16 or wider, within the bound.
No kernel may reach another device: no remote copies, remote signals or barrier semaphores. Data moves between devices by JAX's collectives and lax.ppermute only.
A program may use at most 128 MiB of HBM per device.

v0:
```python
import jax
import jax.numpy as jnp
from jax import lax
from jax.sharding import PartitionSpec as P


def contract_rows(left, right):
    return lax.dot_general(
        left, right, (((0,), (0,)), ((), ())), preferred_element_type=jnp.float32
    )


def contract_cols(left, right):
    return lax.dot_general(
        left, right, (((1,), (1,)), ((), ())), preferred_element_type=jnp.float32
    )


def swiglu_terms(gate, up, hidden_grad):
    sig = jax.nn.sigmoid(gate)
    act = gate * sig
    hidden = (act * up).astype(jnp.bfloat16)
    gate_term = (hidden_grad * up * sig * (1.0 + gate * (1.0 - sig))).astype(jnp.bfloat16)
    up_term = (hidden_grad * act).astype(jnp.bfloat16)
    return (hidden, gate_term, up_term)


def block_work(tok_part, grad_part, gate_full, up_full, down_full):
    gate = jnp.dot(tok_part, gate_full, preferred_element_type=jnp.float32)
    up = jnp.dot(tok_part, up_full, preferred_element_type=jnp.float32)
    hidden_grad = contract_cols(grad_part, down_full)
    hidden, gate_term, up_term = swiglu_terms(gate, up, hidden_grad)
    partial_in = contract_cols(gate_term, gate_full) + contract_cols(up_term, up_full)
    return (hidden, gate_term, up_term, partial_in)


def on_device(tokens, out_grad, gate_weight, up_weight, down_weight):
    gate_full, up_full, down_full = (
        lax.all_gather(gate_weight, "depth", axis=0, tiled=True),
        lax.all_gather(up_weight, "depth", axis=0, tiled=True),
        lax.all_gather(down_weight, "depth", axis=1, tiled=True),
    )
    all_tok, all_grad = (
        lax.all_gather(tokens, "row", axis=0, tiled=True),
        lax.all_gather(out_grad, "row", axis=0, tiled=True),
    )
    hidden, gate_term, up_term, partial_in = block_work(
        all_tok, all_grad, gate_full, up_full, down_full
    )
    input_grad = lax.psum_scatter(
        partial_in, ("row", "col"), scatter_dimension=0, tiled=True
    ).astype(jnp.bfloat16)
    gate_grad, up_grad, down_grad = (
        lax.psum_scatter(
            contract_rows(all_tok, gate_term).astype(jnp.bfloat16),
            "depth",
            scatter_dimension=0,
            tiled=True,
        ).astype(jnp.float32),
        lax.psum_scatter(
            contract_rows(all_tok, up_term).astype(jnp.bfloat16),
            "depth",
            scatter_dimension=0,
            tiled=True,
        ).astype(jnp.float32),
        lax.psum_scatter(
            contract_rows(hidden, all_grad).astype(jnp.bfloat16),
            "depth",
            scatter_dimension=1,
            tiled=True,
        ).astype(jnp.float32),
    )
    return (
        input_grad,
        gate_grad.astype(jnp.bfloat16),
        up_grad.astype(jnp.bfloat16),
        down_grad.astype(jnp.bfloat16),
    )


def solution(mesh):
    return jax.shard_map(
        on_device,
        mesh=mesh,
        in_specs=(
            P(("depth", "row"), None),
            P(("depth", "row"), None),
            P("depth", ("row", "col")),
            P("depth", ("row", "col")),
            P(("row", "col"), "depth"),
        ),
        out_specs=(
            P(("depth", "row", "col"), None),
            P("depth", ("row", "col")),
            P("depth", ("row", "col")),
            P(("row", "col"), "depth"),
        ),
        check_vma=False,
    )
```

profile of v0, /device:TPU:2, one launch (start us, length us, event | category | flops | bytes accessed | tf_op | source)
XLA Modules:
  0.0 703.7 jit_solution(15544658315042769333)
XLA Ops:
  7.2 0.0 all-gather.16.cloned.1.call-start
  7.2 0.7 all-gather.16.cloned.1.call-update
  7.9 0.0 all-gather.14.cloned.1.call-start
  7.9 0.7 all-gather.14.cloned.1.call-update
  8.6 0.0 all-gather.10.cloned.1.call-start
  8.7 0.7 all-gather.10.cloned.1.call-update
  9.4 0.0 all-gather.12.cloned.1.call-start
  9.4 0.5 all-gather.12.cloned.1.call-update
  10.0 0.0 all-gather.8.cloned.1.call-start
  10.0 0.5 all-gather.8.cloned.1.call-update
  10.5 0.0 reduce-scatter.6.cloned.1.call-start
  10.6 103.0 %all-gather.16.cloned.1.call-done = bf16[16,12,8192]{2,1,0:T(8,128)(2,1)} async-done(((bf16[1,12,8192]{2,1,0:T(8,128)(2,1)}), bf16[16,12,8192]{2,1,0:T(8,128)(2,1)}) %all-gather.16.cloned.1.call-update) | async-done | bytes 3145744 | tf_op jit(solution)/shard_map/all_gather | solution.py:44
  113.6 3.2 reshape.11
  116.9 95.9 %all-gather.14.cloned.1.call-done = bf16[16,12,8192]{2,1,0:T(8,128)(2,1)} async-done(((bf16[1,12,8192]{2,1,0:T(8,128)(2,1)}), bf16[16,12,8192]{2,1,0:T(8,128)(2,1)}) %all-gather.14.cloned.1.call-update) | async-done | bytes 3145744 | tf_op jit(solution)/shard_map/all_gather | solution.py:45
  212.7 4.7 reshape.9
  217.4 43.8 %all-gather.10.cloned.1.call-done = bf16[8192,256]{1,0:T(8,128)(2,1)} async-done(((bf16[2048,256]{1,0:T(8,128)(2,1)}), bf16[8192,256]{1,0:T(8,128)(2,1)}) %all-gather.10.cloned.1.call-update) | async-done | bytes 4194320 | tf_op jit(solution)/shard_map/all_gather | solution.py:40
  261.3 3.2 fusion.5
  264.4 49.7 %all-gather.12.cloned.1.call-done = bf16[8192,256]{1,0:T(8,128)(2,1)} async-done(((bf16[2048,256]{1,0:T(8,128)(2,1)}), bf16[8192,256]{1,0:T(8,128)(2,1)}) %all-gather.12.cloned.1.call-update) | async-done | bytes 4194320 | tf_op jit(solution)/shard_map/all_gather | solution.py:39
  314.1 3.2 fusion.6
  317.3 49.7 %all-gather.8.cloned.1.call-done = bf16[256,8192]{1,0:T(8,128)(2,1)} async-done(((bf16[256,2048]{1,0:T(8,128)(2,1)}), bf16[256,8192]{1,0:T(8,128)(2,1)}) %all-gather.8.cloned.1.call-update) | async-done | bytes 4194320 | tf_op jit(solution)/shard_map/all_gather | solution.py:41
  367.0 5.3 multiply_convert_fusion.1
  372.3 0.0 copy-start.3
  372.3 0.6 copy-done.3
  373.0 3.2 fusion.1
  376.2 0.0 reduce-scatter.6.cloned.1.call-update
  376.2 0.0 reduce-scatter.4.cloned.1.call-start
  376.2 4.2 fusion
  380.4 0.0 copy-start.1
  380.4 0.0 reduce-scatter.4.cloned.1.call-update
  380.4 0.0 copy-start.5
  380.4 0.0 reduce-scatter.8.cloned.1.call-start
  380.5 1.8 copy-done.1
  382.3 3.3 convolution_convert_fusion
  385.5 0.0 copy-start.2
  385.5 0.0 reduce-scatter.8.cloned.1.call-update
  385.6 0.0 copy-done.5
  385.6 0.6 dynamic-slice
  386.8 0.0 copy-done.2
  386.8 0.0 copy-start
  386.8 0.0 copy-start.4
  386.8 4.4 fusion.7
  391.2 0.0 copy-done
  391.2 0.0 copy-done.4
  391.2 4.2 convolution_add_fusion
  395.4 296.2 %all-reduce.2 = bf16[192,8192]{1,0:T(8,128)(2,1)S(1)} all-reduce(f32[192,8192]{1,0:T(8,128)} %convolution_add_fusion), channel_id=2, replica_groups=mesh['depth'=4,'row'=16,'col'=4] {'row','col'}, use_global_device_ids=true, to_apply=%region_0.0.clone | all-reduce | flops 1572864 | bytes 9437184
  691.6 0.7 dynamic-slice_convert_fusion
  692.3 2.3 copy.14
  694.6 2.3 copy.13
  (3 shorter events, 0.0 us)
Async XLA Ops:
  7.2 106.4 %all-gather.16.cloned.1.call-start = ((), (), s32[]{:S(2)}) async-start(), calls=%async_computation.10 | async-start | bytes 4456448 | tf_op jit(solution)/shard_map/all_gather | solution.py:44
  7.9 204.8 %all-gather.14.cloned.1.call-start = ((), (), s32[]{:S(2)}) async-start(), calls=%async_computation.9 | async-start | bytes 4456448 | tf_op jit(solution)/shard_map/all_gather | solution.py:45
  8.6 252.6 %all-gather.10.cloned.1.call-start = ((), (), s32[]{:S(2)}) async-start(), calls=%async_computation.4 | async-start | bytes 5242880 | tf_op jit(solution)/shard_map/all_gather | solution.py:40
  9.4 304.7 %all-gather.12.cloned.1.call-start = ((), (), s32[]{:S(2)}) async-start(), calls=%async_computation.5 | async-start | bytes 5242880 | tf_op jit(solution)/shard_map/all_gather | solution.py:39
  10.0 357.0 %all-gather.8.cloned.1.call-start = ((), (), s32[]{:S(2)}) async-start(), calls=%async_computation.3 | async-start | bytes 5242880 | tf_op jit(solution)/shard_map/all_gather | solution.py:41
  10.5 681.7 %reduce-scatter.6.cloned.1.call-start = ((), (), s32[]{:S(2)}) async-start(), calls=%async_computation.7 | async-start | bytes 5242880 | tf_op jit(solution)/shard_map/reduce_scatter | solution.py:60
  372.3 0.6 copy-start.3
  376.2 318.4 %reduce-scatter.4.cloned.1.call-start = ((), (), s32[]{:S(2)}) async-start(), calls=%async_computation.6 | async-start | bytes 5242880 | tf_op jit(solution)/shard_map/reduce_scatter | solution.py:54
  380.4 1.9 copy-start.1
  380.4 5.1 copy-start.5
  380.4 316.4 %reduce-scatter.8.cloned.1.call-start = ((), (), s32[]{:S(2)}) async-start(), calls=%async_computation.8 | async-start | bytes 5242880 | tf_op jit(solution)/shard_map/reduce_scatter | solution.py:66
  385.5 1.3 copy-start.2
  386.8 4.4 copy-start
  386.8 4.4 copy-start.4
Sparse Core Ops, SparseCore 0:
  10.6 102.9 all-gather.15
  116.2 96.5 all-gather.13
  214.6 46.6 all-gather.9
  262.9 51.1 all-gather.11
  315.8 51.1 all-gather.7
  376.3 49.0 reduce-scatter.5
  428.2 49.0 reduce-scatter.3
  480.4 49.0 reduce-scatter.7
where the time goes:
time: 704 us
  waiting for transfers between devices  345 us (49%)
  blocking collectives  296 us (42%)
  matrix products  30.8 us (4%)
  local copies, waits for them, and re-layouts  16.2 us (2%)
  between operations  14.9 us (2%)
    unnamed x1, blocking collectives  296 us
    all_gather x1, waiting for transfers between devices, on_device(): lax.all_gather(tokens, 'row', axis=0, tiled=True)  103 us
    all_gather x1, waiting for transfers between devices, on_device(): lax.all_gather(out_grad, 'row', axis=0, tiled=True)  95.9 us
    all_gather x1, waiting for transfers between devices, on_device(): lax.all_gather(gate_weight, 'depth', axis=0, tiled=True)  49.7 us
    all_gather x1, waiting for transfers between devices, on_device(): lax.all_gather(down_weight, 'depth', axis=1, tiled=True)  49.7 us
    all_gather x1, waiting for transfers between devices, on_device(): lax.all_gather(up_weight, 'depth', axis=0, tiled=True)  43.8 us
    unnamed x17, local copies, waits for them, and re-layouts  15.5 us
  transfers between devices with their start and end apart: 8, of which 5 were waited for; matrix products, arithmetic and copies ran while one was open for 5% of the time, Pallas kernels for 0%

commit v1 on v0

--- a/solution.py
+++ b/solution.py
@@ -1,7 +1,19 @@
+import functools
 import jax
 import jax.numpy as jnp
 from jax import lax
 from jax.sharding import PartitionSpec as P
+
+
+def end_trees(view, group_axis):
+    cards = []
+    for _ in range(lax.axis_size(group_axis)):
+        cards.append(view)
+    value_now = jnp.concatenate(cards, axis=1)
+    return lax.all_to_all(value_now, group_axis, 1, 1, tiled=True)
+
+
+solve_bars_up = functools.partial(end_trees, group_axis="depth")
 
 
 def contract_rows(left, right):
@@ -38,7 +50,7 @@
     gate_full, up_full, down_full = (
         lax.all_gather(gate_weight, "depth", axis=0, tiled=True),
         lax.all_gather(up_weight, "depth", axis=0, tiled=True),
-        lax.all_gather(down_weight, "depth", axis=1, tiled=True),
+        solve_bars_up(down_weight),
     )
     all_tok, all_grad = (
         lax.all_gather(tokens, "row", axis=0, tiled=True),

time: 704 us -> 652 us (0.926)
  waiting for transfers between devices: 345 us -> 226 us
  blocking collectives: 296 us -> 350 us
  local copies, waits for them, and re-layouts: 16.2 us -> 31.2 us
    all_gather x1, waiting for transfers between devices: 103 us -> 33.8 us  [on_device(): lax.all_gather(tokens, 'row', axis=0, tiled=True)]
    all_to_all x0 -> x1, blocking collectives: none -> 53.7 us  [end_trees(): return lax.all_to_all(value_now, group_axis, 1, 1, tiled=True)]
    all_gather x1 -> x0, waiting for transfers between devices: 49.7 us -> none  [on_device(): lax.all_gather(down_weight, 'depth', axis=1, tiled=True)]
    all_to_all x0 -> x2, local copies, waits for them, and re-layouts: none -> 12.5 us  [end_trees(): return lax.all_to_all(value_now, group_axis, 1, 1, tiled=True)]
    unnamed x17 -> x22, local copies, waits for them, and re-layouts: 15.5 us -> 18.1 us
  transfers between devices with their start and end apart: 8 -> 7, of which waited for: 5 -> 4; matrix products, arithmetic and copies ran while one was open for 5% -> 8% of each run, Pallas kernels for 0% -> 0%
where the time goes in v1:
time: 652 us; the launch traced here: 651 us
  blocking collectives  350 us (54%)
  waiting for transfers between devices  226 us (35%)
  local copies, waits for them, and re-layouts  31.2 us (5%)
  matrix products  27.2 us (4%)
  between operations  14.9 us (2%)
    unnamed x1, blocking collectives  296 us
    all_gather x1, waiting for transfers between devices, on_device(): lax.all_gather(out_grad, 'row', axis=0, tiled=True)  95.9 us
    all_to_all x1, blocking collectives, end_trees(): return lax.all_to_all(value_now, group_axis, 1, 1, tiled=True)  53.7 us
    all_gather x1, waiting for transfers between devices, on_device(): lax.all_gather(gate_weight, 'depth', axis=0, tiled=True)  49.7 us
    all_gather x1, waiting for transfers between devices, on_device(): lax.all_gather(up_weight, 'depth', axis=0, tiled=True)  43.8 us
    all_gather x1, waiting for transfers between devices, on_device(): lax.all_gather(tokens, 'row', axis=0, tiled=True)  33.8 us
    unnamed x22, local copies, waits for them, and re-layouts  18.1 us
  transfers between devices with their start and end apart: 7, of which 4 were waited for; matrix products, arithmetic and copies ran while one was open for 8% of the time, Pallas kernels for 0%

profile of v1, /device:TPU:2, one launch (start us, length us, event | category | flops | bytes accessed | tf_op | source)
XLA Modules:
  0.0 651.5 jit_solution(15861888783106214801)
XLA Ops:
  7.2 0.0 all-gather.13.cloned.1.call-start
  7.2 0.7 all-gather.13.cloned.1.call-update
  7.9 0.0 all-gather.11.cloned.1.call-start
  7.9 0.7 all-gather.11.cloned.1.call-update
  8.6 0.0 all-gather.7.cloned.1.call-start
  8.7 0.7 all-gather.7.cloned.1.call-update
  9.4 0.0 all-gather.9.cloned.1.call-start
  9.4 0.5 all-gather.9.cloned.1.call-update
  10.0 0.0 reduce-scatter.4.cloned.1.call-start
  10.0 1.5 copy.15
  11.5 2.2 pad_maximum_fusion
  13.7 6.2 copy.19
  19.9 53.7 %all_to_all.12 = bf16[256,4,2048]{2,0,1:T(8,128)(2,1)} all-to-all(bf16[256,4,2048]{2,0,1:T(8,128)(2,1)} %copy.19), channel_id=1, replica_groups=mesh['depth'=4,'row'=16,'col'=4] {'depth'}, dimensions={1} | all-to-all | bytes 8388608 | tf_op jit(solution)/shard_map/all_to_all | solution.py:13
  73.6 6.2 copy.20
  79.8 33.8 %all-gather.13.cloned.1.call-done = bf16[16,12,8192]{2,1,0:T(8,128)(2,1)} async-done(((bf16[1,12,8192]{2,1,0:T(8,128)(2,1)}), bf16[16,12,8192]{2,1,0:T(8,128)(2,1)}) %all-gather.13.cloned.1.call-update) | async-done | bytes 3145744 | tf_op jit(solution)/shard_map/all_gather | solution.py:56
  113.6 3.2 reshape.13
  116.9 95.9 %all-gather.11.cloned.1.call-done = bf16[16,12,8192]{2,1,0:T(8,128)(2,1)} async-done(((bf16[1,12,8192]{2,1,0:T(8,128)(2,1)}), bf16[16,12,8192]{2,1,0:T(8,128)(2,1)}) %all-gather.11.cloned.1.call-update) | async-done | bytes 3145744 | tf_op jit(solution)/shard_map/all_gather | solution.py:57
  212.7 4.7 reshape.11
  217.4 43.8 %all-gather.7.cloned.1.call-done = bf16[8192,256]{1,0:T(8,128)(2,1)} async-done(((bf16[2048,256]{1,0:T(8,128)(2,1)}), bf16[8192,256]{1,0:T(8,128)(2,1)}) %all-gather.7.cloned.1.call-update) | async-done | bytes 4194320 | tf_op jit(solution)/shard_map/all_gather | solution.py:52
  261.3 3.2 fusion.5
  264.4 49.7 %all-gather.9.cloned.1.call-done = bf16[8192,256]{1,0:T(8,128)(2,1)} async-done(((bf16[2048,256]{1,0:T(8,128)(2,1)}), bf16[8192,256]{1,0:T(8,128)(2,1)}) %all-gather.9.cloned.1.call-update) | async-done | bytes 4194320 | tf_op jit(solution)/shard_map/all_gather | solution.py:51
  314.1 3.3 fusion.6
  317.4 0.0 copy-done.1
  317.5 1.1 copy-done.3
  318.5 1.6 multiply_convert_fusion.1
  320.2 0.6 copy-done.4
  320.8 3.2 fusion
  324.0 0.0 reduce-scatter.4.cloned.1.call-update
  324.1 0.0 reduce-scatter.6.cloned.1.call-start
  324.1 4.1 fusion.1
  328.2 0.0 reduce-scatter.6.cloned.1.call-update
  328.2 0.0 copy-start.7
  328.3 0.0 reduce-scatter.8.cloned.1.call-start
  328.3 1.8 copy-done.2
  330.1 3.3 convolution_convert_fusion
  333.4 0.0 reduce-scatter.8.cloned.1.call-update
  333.4 0.6 dynamic-slice
  334.6 0.0 copy-done.5
  334.7 0.0 copy-start
  334.7 0.0 copy-start.6
  334.7 4.3 fusion.7
  339.0 0.0 copy-done
  339.0 0.0 copy-done.6
  339.0 4.2 convolution_add_fusion
  343.2 296.2 %all-reduce.2 = bf16[192,8192]{1,0:T(8,128)(2,1)S(1)} all-reduce(f32[192,8192]{1,0:T(8,128)} %convolution_add_fusion), channel_id=2, replica_groups=mesh['depth'=4,'row'=16,'col'=4] {'row','col'}, use_global_device_ids=true, to_apply=%region_0.0.clone | all-reduce | flops 1572864 | bytes 9437184
  639.4 0.7 dynamic-slice_convert_fusion
  640.1 2.3 copy.21
  642.4 2.3 copy.22
  (9 shorter events, 0.0 us)
Async XLA Ops:
  7.2 106.4 %all-gather.13.cloned.1.call-start = ((), (), s32[]{:S(2)}) async-start(), calls=%async_computation.10 | async-start | bytes 4456448 | tf_op jit(solution)/shard_map/all_gather | solution.py:56
  7.9 204.8 %all-gather.11.cloned.1.call-start = ((), (), s32[]{:S(2)}) async-start(), calls=%async_computation.9 | async-start | bytes 4456448 | tf_op jit(solution)/shard_map/all_gather | solution.py:57
  8.6 252.6 %all-gather.7.cloned.1.call-start = ((), (), s32[]{:S(2)}) async-start(), calls=%async_computation.4 | async-start | bytes 5242880 | tf_op jit(solution)/shard_map/all_gather | solution.py:52
  9.4 304.7 %all-gather.9.cloned.1.call-start = ((), (), s32[]{:S(2)}) async-start(), calls=%async_computation.5 | async-start | bytes 5242880 | tf_op jit(solution)/shard_map/all_gather | solution.py:51
  10.0 630.2 %reduce-scatter.4.cloned.1.call-start = ((), (), s32[]{:S(2)}) async-start(), calls=%async_computation.6 | async-start | bytes 5242880 | tf_op jit(solution)/shard_map/reduce_scatter | solution.py:66
  314.1 3.3 copy-start.1
  314.1 4.4 copy-start.3
  320.2 0.6 copy-start.4
  324.1 318.3 %reduce-scatter.6.cloned.1.call-start = ((), (), s32[]{:S(2)}) async-start(), calls=%async_computation.7 | async-start | bytes 5242880 | tf_op jit(solution)/shard_map/reduce_scatter | solution.py:72
  328.2 1.9 copy-start.2
  328.2 5.2 copy-start.7
  328.3 316.4 %reduce-scatter.8.cloned.1.call-start = ((), (), s32[]{:S(2)}) async-start(), calls=%async_computation.8 | async-start | bytes 5242880 | tf_op jit(solution)/shard_map/reduce_scatter | solution.py:78
  333.4 1.3 copy-start.5
  334.7 4.3 copy-start
  334.7 4.3 copy-start.6
Sparse Core Ops, SparseCore 0:
  10.6 102.9 all-gather.12
  116.2 96.5 all-gather.10
  214.6 46.6 all-gather.6
  262.9 51.1 all-gather.8
  324.2 49.0 reduce-scatter.3
  375.9 49.1 reduce-scatter.5
  428.2 49.0 reduce-scatter.7
